TPU v7x, 256 devices: a whole 4x4x8 slice. The times are simulated.
256 devices in a mesh: dp: 128 (over z, y, x), sub: 2 (over core).
Axes of the slice: x: 4, y: 4, z: 8, core: 2. Of those that a mesh axis runs over, the one named last changes fastest.
Arguments:
- grads: bfloat16 [128, 2, 2048, 512], P('dp', None, 'sub'), may hold values from -84 to 84
- errors: bfloat16 [128, 2, 2048, 512], P('dp', None, 'sub'), may hold values from -3 to 3
- vec_grads: float32 [128, 2, 2048], P('dp', None, 'sub'), may hold values from -24 to 24
- gains: float32 [2, 2048], P(None, 'sub'), may hold values from 0.5 to 1.5
- q_start: float32 [2, 512, 32], replicated, may hold values from -0.25 to 0.25
- owner: int32 [256], replicated, may hold values from 0 to 127, as said below
- momentum: float32 [512, 16, 512], P('dp', None, 'sub'), may hold values from -3 to 3
- master: float32 [512, 16, 512], P('dp', None, 'sub'), may hold values from -5 to 5
Outputs:
- errors_out: bfloat16 [128, 2, 2048, 512], P('dp', None, 'sub')
- new_gains: float32 [2, 2048], P(None, 'sub')
- new_momentum: float32 [512, 16, 512], P('dp', None, 'sub')
- new_master: float32 [512, 16, 512], P('dp', None, 'sub')
- weights: bfloat16 [2, 2048, 512], P(None, None, 'sub')
Inputs may be any that keep to these rules, and one draw needn't show every extreme that they name: `owner`: each dp index owns at most 4 blocks and some index owns exactly 4; momentum and master in empty slots are not used.
All inputs are finite; a program needn't handle non-finite values.
Results may differ from a plain program's by a relative error of at most 0.005.
Values may be sent and summed in bfloat16 or wider, within the bound.
A program may use at most 128 MiB of HBM per device.

v0:
```python
import jax
import jax.numpy as jnp
from jax import lax
from jax.sharding import PartitionSpec as P

ROUNDS = 2
HIGH = lax.Precision.HIGHEST
momentum_decay = 0.9
step_rate = 0.5
vector_rate = 1.0


def solve_basis(left, gram):
    lower = jnp.linalg.cholesky(gram)
    return lax.linalg.triangular_solve(lower, left, left_side=False, lower=True, transpose_a=True)


def body(grads, errors, vec_grads, gains, q_start, owner, momentum, master):
    replicas = lax.axis_size("dp")
    slots = momentum.shape[0]
    rows_block = momentum.shape[1]
    half_cols = momentum.shape[2]
    blocks = owner.shape[0]
    mixed = grads[0].astype(jnp.float32) + errors[0].astype(jnp.float32)
    mats = mixed.shape[0]
    vec_total = lax.psum(vec_grads[0], "dp")
    new_gains = gains - vector_rate * (vec_total / replicas)
    right = q_start
    for step_index in range(ROUNDS):
        local_left = jnp.einsum("mdk,mkr->mdr", mixed, right, precision=HIGH)
        left = lax.psum(local_left, "dp") / replicas
        gram = lax.psum(jnp.einsum("mdr,mds->mrs", left, left, precision=HIGH), "sub")
        basis = solve_basis(left, gram)
        local_right = jnp.einsum("mdk,mdr->mkr", mixed, basis, precision=HIGH)
        right = lax.psum(local_right, ("dp", "sub")) / replicas
    approx_local = jnp.einsum("mdr,mkr->mdk", basis, right, precision=HIGH)
    errors_out = (mixed - approx_local).astype(jnp.bfloat16)[None]
    basis_full = lax.all_gather(basis.astype(jnp.bfloat16), "sub", axis=1, tiled=True).astype(
        basis.dtype
    )
    right_half = lax.dynamic_slice_in_dim(right, lax.axis_index("sub") * half_cols, half_cols, 1)
    approx_half = jnp.einsum("mdr,mkr->mdk", basis_full, right_half, precision=HIGH)
    full_rows = basis_full.shape[1]
    approx_blocks = approx_half.reshape(blocks, rows_block, half_cols)
    index = jnp.arange(blocks, dtype=jnp.int32)
    same = owner[:, None] == owner[None, :]
    earlier = index[None, :] < index[:, None]
    rank = jnp.sum((same & earlier).astype(jnp.int32), axis=1)
    pos = owner * slots + rank
    mine = (owner[None, :] == lax.axis_index("dp")) & (
        rank[None, :] == jnp.arange(slots, dtype=jnp.int32)[:, None]
    )
    mine_int = mine.astype(jnp.int32)
    local_block = jnp.sum(mine_int * index[None, :], axis=1)
    valid = jnp.sum(mine_int, axis=1).astype(jnp.float32)[:, None, None]
    approx_slots = approx_blocks[local_block] * valid
    new_momentum = (momentum_decay * momentum + approx_slots) * valid
    new_master = (master - step_rate * new_momentum) * valid
    gathered = lax.all_gather(new_master.astype(jnp.bfloat16), "dp", axis=0, tiled=True)
    weights = gathered[pos].reshape(mats, full_rows, half_cols)
    return (errors_out, new_gains, new_momentum, new_master, weights)


def solution(mesh):
    placed = (
        P("dp", None, "sub", None),
        P("dp", None, "sub", None),
        P("dp", None, "sub"),
        P(None, "sub"),
        P(),
        P(),
        P("dp", None, "sub"),
        P("dp", None, "sub"),
    )
    return jax.shard_map(
        body,
        mesh=mesh,
        in_specs=placed,
        out_specs=(
            P("dp", None, "sub", None),
            P(None, "sub"),
            P("dp", None, "sub"),
            P("dp", None, "sub"),
            P(None, None, "sub"),
        ),
        check_vma=False,
    )
```

profile of v0, /device:TPU:2, one launch (start us, length us, event | category | flops | bytes accessed | tf_op | source)
XLA Modules:
  0.0 1345.0 jit_solution(2822538106656851169)
XLA Ops:
  8.1 7.2 fusion.6
  15.6 215.6 %all-reduce.5.cloned.1.call-done = f32[2,1024,32]{1,2,0:T(8,128)} async-done(((f32[2,1024,32]{1,2,0:T(8,128)}), f32[2,1024,32]{1,2,0:T(8,128)}) %all-reduce.5.cloned.1.call-update) | async-done | bytes 262160 | tf_op jit(solution)/shard_map/psum | solution.py:31
  231.1 1.4 fusion.15
  232.5 3.4 psum.50
  236.0 5.9 custom-call.8
  242.1 4.9 custom-call.9
  247.1 1.4 convolution_bitcast_fusion.1
  248.5 5.2 fusion.4
  253.9 239.2 %all-reduce.7.cloned.1.call-done = f32[2,512,32]{1,2,0:T(8,128)} async-done(((f32[2,512,32]{1,2,0:T(8,128)}), f32[2,512,32]{1,2,0:T(8,128)}) %all-reduce.7.cloned.1.call-update) | async-done | bytes 131088 | tf_op jit(solution)/shard_map/psum | solution.py:35
  493.1 6.6 fusion.2
  499.8 209.7 %all-reduce.9.cloned.1.call-done = f32[2,1024,32]{1,2,0:T(8,128)} async-done(((f32[2,1024,32]{1,2,0:T(8,128)}), f32[2,1024,32]{1,2,0:T(8,128)}) %all-reduce.9.cloned.1.call-update) | async-done | bytes 262160 | tf_op jit(solution)/shard_map/psum | solution.py:31
  709.5 1.4 fusion.12
  710.9 3.6 psum.53
  714.6 5.9 custom-call.10
  720.7 4.9 custom-call.11
  725.6 1.4 fusion.38
  727.0 5.3 fusion
  732.4 2.0 all_gather.6
  734.4 237.4 %all-reduce.11.cloned.1.call-done = f32[2,512,32]{1,2,0:T(8,128)} async-done(((f32[2,512,32]{1,2,0:T(8,128)}), f32[2,512,32]{1,2,0:T(8,128)}) %all-reduce.11.cloned.1.call-update) | async-done | bytes 131088 | tf_op jit(solution)/shard_map/psum | solution.py:35
  972.8 3.8 fusion.22
  976.5 2.7 gather_fusion
  980.1 347.4 %psum.55 = f32[2,1024]{1,0:T(2,128)S(1)} all-reduce(f32[2,1024]{1,0:T(2,128)S(1)} %bitcast.54), channel_id=1, replica_groups=mesh['dp'=128,'sub'=2] {'dp'}, use_global_device_ids=true, to_apply=%region_8.11 | all-reduce | flops 2048 | bytes 16384 | tf_op jit(solution)/shard_map/psum | solution.py:26
  1328.1 6.1 fusion.9
  1334.2 4.3 gather_fusion.1
  (50 shorter events, 4.5 us)
Async XLA Ops:
  7.2 0.9 copy-start
  7.2 241.3 %copy-start.1 = (bf16[1,2,1024,512]{3,2,1,0:T(8,128)(2,1)S(1)}, bf16[1,2,1024,512]{3,2,1,0:T(8,128)(2,1)}, u32[]{:S(2)}) copy-start(bf16[1,2,1024,512]{3,2,1,0:T(8,128)(2,1)} %param.12) | copy-start | bytes 6291460
  7.2 8.2 copy-start.5
  7.2 223.9 %all-reduce.5.cloned.1.call-start = ((), (), s32[]{:S(2)}) async-start(), calls=%async_computation | async-start | bytes 524288 | tf_op jit(solution)/shard_map/psum | solution.py:31
  15.3 477.8 %all-reduce.7.cloned.1.call-start = ((), (), s32[]{:S(2)}) async-start(), calls=%async_computation.1 | async-start | bytes 262144 | tf_op jit(solution)/shard_map/psum | solution.py:35
  253.7 455.8 %all-reduce.9.cloned.1.call-start = ((), (), s32[]{:S(2)}) async-start(), calls=%async_computation.2 | async-start | bytes 524288 | tf_op jit(solution)/shard_map/psum | solution.py:31
  499.7 472.0 %all-reduce.11.cloned.1.call-start = ((), (), s32[]{:S(2)}) async-start(), calls=%async_computation.3 | async-start | bytes 262144 | tf_op jit(solution)/shard_map/psum | solution.py:35
  727.0 252.3 %copy-start.3 = (f32[4,16,256]{2,1,0:T(8,128)S(1)}, f32[4,16,256]{2,1,0:T(8,128)}, u32[]{:S(2)}) copy-start(f32[4,16,256]{2,1,0:T(8,128)} %param.18) | copy-start | bytes 196612
  727.0 252.3 %copy-start.4 = (f32[4,16,256]{2,1,0:T(8,128)S(1)}, f32[4,16,256]{2,1,0:T(8,128)}, u32[]{:S(2)}) copy-start(f32[4,16,256]{2,1,0:T(8,128)} %param.17) | copy-start | bytes 196612
  727.0 253.1 %copy-start.7 = (f32[1,2,1024]{2,1,0:T(2,128)S(1)}, f32[1,2,1024]{2,1,0:T(2,128)}, u32[]{:S(2)}) copy-start(f32[1,2,1024]{2,1,0:T(2,128)} %param.13) | copy-start | bytes 24580
  727.0 600.5 %copy-start.6 = (f32[2,1024]{1,0:T(2,128)S(1)}, f32[2,1024]{1,0:T(2,128)}, u32[]{:S(2)}) copy-start(f32[2,1024]{1,0:T(2,128)} %param.14) | copy-start | bytes 24580
  732.3 601.9 %all-gather.2.cloned.1.call-start = ((), (), s32[]{:S(2)}) async-start(), calls=%async_computation.4 | async-start | bytes 4227072 | tf_op jit(solution)/shard_map/all_gather | solution.py:59
  971.8 356.3 %copy-start.2 = (f32[2,512,32]{1,2,0:T(8,128)S(1)}, f32[2,512,32]{1,2,0:T(8,128)}, u32[]{:S(2)}) copy-start(f32[2,512,32]{1,2,0:T(8,128)} %all-reduce.11.cloned.1.call-done) | copy-start | bytes 393220
Sparse Core Ops, SparseCore 0:
  15.4 215.6 all-reduce.4
  253.8 239.2 all-reduce.6
  500.0 209.4 all-reduce.8
  732.5 239.2 all-reduce.10
  980.2 113.5 all-gather.1
where the time goes:
time: 1350 us
  waiting for transfers between devices  902 us (67%)
  blocking collectives  356 us (26%)
  matrix products  39.8 us (3%)
  other arithmetic  24.7 us (2%)
  between operations  14 us (1%)
    psum x2, waiting for transfers between devices, body(): right = lax.psum(local_right, ('dp', 'sub')) / replicas  477 us
    psum x2, waiting for transfers between devices, body(): left = lax.psum(local_left, 'dp') / replicas  425 us
    psum x1, blocking collectives, body(): vec_total = lax.psum(vec_grads[0], 'dp')  347 us
  transfers between devices with their start and end apart: 5, of which 4 were waited for; matrix products, arithmetic and copies ran while one was open for 1% of the time, Pallas kernels for 0%

commit v1 on v0

--- a/solution.py
+++ b/solution.py
@@ -32,7 +32,7 @@
         gram = lax.psum(jnp.einsum("mdr,mds->mrs", left, left, precision=HIGH), "sub")
         basis = solve_basis(left, gram)
         local_right = jnp.einsum("mdk,mdr->mkr", mixed, basis, precision=HIGH)
-        right = lax.psum(local_right, ("dp", "sub")) / replicas
+        right = jnp.sum(lax.all_gather(local_right, ("dp", "sub")), axis=0) / replicas
     approx_local = jnp.einsum("mdr,mkr->mdk", basis, right, precision=HIGH)
     errors_out = (mixed - approx_local).astype(jnp.bfloat16)[None]
     basis_full = lax.all_gather(basis.astype(jnp.bfloat16), "sub", axis=1, tiled=True).astype(

time: 1350 us -> 1190 us (0.88)
  waiting for transfers between devices: 902 us -> 723 us
  other arithmetic: 24.7 us -> 47.9 us
    psum x2 -> x0, waiting for transfers between devices: 477 us -> none  [body(): right = lax.psum(local_right, ('dp', 'sub')) / replicas]
    all_gather x0 -> x2, waiting for transfers between devices: none -> 297 us  [body(): lax.all_gather(local_right, ('dp', 'sub'))]
    reduce_sum x0 -> x2, other arithmetic: none -> 24.1 us  [body(): jnp.sum(lax.all_gather(local_right, ('dp', 'sub')), axis=0) / replicas]
where the time goes in v1:
time: 1190 us
  waiting for transfers between devices  723 us (61%)
  blocking collectives  356 us (30%)
  other arithmetic  47.9 us (4%)
  matrix products  39.7 us (3%)
  between operations  14 us (1%)
    psum x2, waiting for transfers between devices, body(): left = lax.psum(local_left, 'dp') / replicas  426 us
    psum x1, blocking collectives, body(): vec_total = lax.psum(vec_grads[0], 'dp')  347 us
    all_gather x2, waiting for transfers between devices, body(): lax.all_gather(local_right, ('dp', 'sub'))  297 us
    reduce_sum x2, other arithmetic, body(): jnp.sum(lax.all_gather(local_right, ('dp', 'sub')), axis=0) / replicas  24.1 us
  transfers between devices with their start and end apart: 5, of which 4 were waited for; matrix products, arithmetic and copies ran while one was open for 1% of the time, Pallas kernels for 0%

profile of v1, /device:TPU:2, one launch (start us, length us, event | category | flops | bytes accessed | tf_op | source)
XLA Modules:
  0.0 1189.1 jit_solution(15336198972621357288)
XLA Ops:
  8.1 7.2 fusion.6
  15.4 215.8 %all-reduce.3.cloned.1.call-done = f32[2,1024,32]{1,2,0:T(8,128)} async-done(((f32[2,1024,32]{1,2,0:T(8,128)}), f32[2,1024,32]{1,2,0:T(8,128)}) %all-reduce.3.cloned.1.call-update) | async-done | bytes 262160 | tf_op jit(solution)/shard_map/psum | solution.py:31
  231.2 1.4 fusion.15
  232.6 3.4 psum.36
  236.1 5.9 custom-call.8
  242.2 4.9 custom-call.9
  248.5 5.2 fusion.4
  253.8 149.5 %all-gather.8.cloned.1.call-done = f32[512,512,32]{1,2,0:T(8,128)} async-done(((f32[2,512,32]{1,2,0:T(8,128)}), f32[512,512,32]{1,2,0:T(8,128)}) %all-gather.8.cloned.1.call-update) | async-done | bytes 33554448 | tf_op jit(solution)/shard_map/all_gather | solution.py:35
  403.3 12.1 %reduce_sum.47 = f32[2,512,32]{1,2,0:T(8,128)S(1)} reduce(f32[256,2,512,32]{2,3,1,0:T(8,128)} %bitcast.55, f32[]{:T(128)} %constant.57.clone.1), dimensions={0}, to_apply=%region_4.7 | reduce | flops 8355840 | bytes 33685508 | tf_op jit(solution)/shard_map/reduce_sum | solution.py:35
  415.4 6.6 fusion.2
  422.2 210.3 %all-reduce.5.cloned.1.call-done = f32[2,1024,32]{1,2,0:T(8,128)} async-done(((f32[2,1024,32]{1,2,0:T(8,128)}), f32[2,1024,32]{1,2,0:T(8,128)}) %all-reduce.5.cloned.1.call-update) | async-done | bytes 262160 | tf_op jit(solution)/shard_map/psum | solution.py:31
  632.5 1.4 fusion.12
  633.9 3.4 psum.38
  637.4 5.9 custom-call.10
  643.5 4.9 custom-call.11
  649.8 5.2 fusion
  655.5 2.0 all_gather.22
  657.5 147.1 %all-gather.10.cloned.1.call-done = f32[512,512,32]{1,2,0:T(8,128)} async-done(((f32[2,512,32]{1,2,0:T(8,128)}), f32[512,512,32]{1,2,0:T(8,128)}) %all-gather.10.cloned.1.call-update) | async-done | bytes 33554448 | tf_op jit(solution)/shard_map/all_gather | solution.py:35
  804.6 12.1 %reduce_sum.48 = f32[2,512,32]{1,2,0:T(8,128)S(1)} reduce(f32[256,2,512,32]{2,3,1,0:T(8,128)} %bitcast.54, f32[]{:T(128)} %constant.57.clone.1), dimensions={0}, to_apply=%region_7.10 | reduce | flops 8355840 | bytes 33685508 | tf_op jit(solution)/shard_map/reduce_sum | solution.py:35
  816.7 3.8 fusion.22
  820.5 2.7 gather_fusion
  824.1 347.5 %psum.39 = f32[2,1024]{1,0:T(2,128)S(1)} all-reduce(f32[2,1024]{1,0:T(2,128)S(1)} %bitcast.58), channel_id=1, replica_groups=mesh['dp'=128,'sub'=2] {'dp'}, use_global_device_ids=true, to_apply=%region_8.11 | all-reduce | flops 2048 | bytes 16384 | tf_op jit(solution)/shard_map/psum | solution.py:26
  1172.2 6.1 fusion.9
  1178.3 4.3 gather_fusion.1
  (52 shorter events, 6.5 us)
Async XLA Ops:
  7.2 0.9 copy-start
  7.2 241.3 %copy-start.2 = (bf16[1,2,1024,512]{3,2,1,0:T(8,128)(2,1)S(1)}, bf16[1,2,1024,512]{3,2,1,0:T(8,128)(2,1)}, u32[]{:S(2)}) copy-start(bf16[1,2,1024,512]{3,2,1,0:T(8,128)(2,1)} %param.12) | copy-start | bytes 6291460
  7.2 224.0 %all-reduce.3.cloned.1.call-start = ((), (), s32[]{:S(2)}) async-start(), calls=%async_computation | async-start | bytes 524288 | tf_op jit(solution)/shard_map/psum | solution.py:31
  15.3 388.0 %all-gather.8.cloned.1.call-start = ((), (), s32[]{:S(2)}) async-start(), calls=%async_computation.3 | async-start | bytes 33685504 | tf_op jit(solution)/shard_map/all_gather | solution.py:35
  253.8 378.7 %all-reduce.5.cloned.1.call-start = ((), (), s32[]{:S(2)}) async-start(), calls=%async_computation.1 | async-start | bytes 524288 | tf_op jit(solution)/shard_map/psum | solution.py:31
  422.0 233.2 %copy-start.5 = (s32[256]{0:T(256)S(1)}, s32[256]{0:T(256)}, u32[]{:S(2)}) copy-start(s32[256]{0:T(256)} %param.16) | copy-start | bytes 3076
  422.0 382.6 %all-gather.10.cloned.1.call-start = ((), (), s32[]{:S(2)}) async-start(), calls=%async_computation.4 | async-start | bytes 33685504 | tf_op jit(solution)/shard_map/all_gather | solution.py:35
  655.1 523.2 %all-gather.6.cloned.1.call-start = ((), (), s32[]{:S(2)}) async-start(), calls=%async_computation.2 | async-start | bytes 4227072 | tf_op jit(solution)/shard_map/all_gather | solution.py:59
  816.7 6.6 copy-start.3
  816.7 6.6 copy-start.4
  816.7 7.4 copy-start.7
  816.7 354.8 %copy-start.6 = (f32[2,1024]{1,0:T(2,128)S(1)}, f32[2,1024]{1,0:T(2,128)}, u32[]{:S(2)}) copy-start(f32[2,1024]{1,0:T(2,128)} %param.14) | copy-start | bytes 24580
  1171.6 11.0 copy-start.1
Sparse Core Ops, SparseCore 0:
  15.4 215.7 all-reduce.2
  253.9 149.3 all-gather.7
  422.1 210.3 all-reduce.4
  655.2 149.3 all-gather.9
  824.2 114.4 all-gather.5
